TPU v7x, 128 devices: a whole 4x4x4 slice. The times are simulated.
128 devices in a mesh: pipe: 4 (over y), dp: 32 (over z, x, core).
Axes of the slice: x: 4, y: 4, z: 4, core: 2. Of those that a mesh axis runs over, the one named last changes fastest.
Arguments:
- x_in: bfloat16 [4, 1024, 4096], P(None, 'dp'), may hold values from -6 to 6
- cotangent: bfloat16 [4, 1024, 4096], P(None, 'dp'), may hold values from -6 to 6
- weights: bfloat16 [4, 64, 64, 2048], P('pipe', 'dp'), as said below
- live_rows: int32 [4, 64, 32], P('pipe'), may hold values from 0 to 63, as said below
- moment: float32 [4, 64, 64, 2048], P('pipe', 'dp'), may hold values from -0.125 to 0.125
- second: float32 [4, 64, 64, 2048], P('pipe', 'dp'), may hold values from 1.2207031e-05 to 0.00024414062
Outputs:
- weights_out: bfloat16 [4, 64, 64, 2048], P('pipe', 'dp')
- moment_out: float32 [4, 64, 64, 2048], P('pipe', 'dp')
- second_out: float32 [4, 64, 64, 2048], P('pipe', 'dp')
Inputs may be any that keep to these rules, and one draw needn't show every extreme that they name: `live_rows`: for each layer and block column the 32 entries are distinct block rows. `weights`: entry [l, j, b, k * 64 + a] is the weight from input feature live_rows[l, j, k] * 64 + a to output feature j * 64 + b; unstored blocks are zero.
All inputs are finite; a program needn't handle non-finite values.
Results may differ from a plain program's by a relative error of at most 0.009.
Values may be sent and summed in bfloat16 or wider, within the bound.
A program may use at most 256 MiB of HBM per device.

v0:
```python
import math
import jax
import jax.numpy as jnp
from jax import lax
from jax.sharding import PartitionSpec as P

HEAD = 128
column_group = 8


def shifted(value, axis, steps):
    count = lax.axis_size(axis)
    leading, last = (max(0, -steps), min(count, count - steps))
    return lax.ppermute(value, axis, [(source, source + steps) for source in range(leading, last)])


def shrink(magnitude, threshold):
    return jnp.maximum(magnitude - threshold, 0.0) / jnp.maximum(magnitude, threshold)


def column_products(normed, section_weights, live_index):
    tokens, features = normed.shape
    column_count, block_size, wide = section_weights.shape
    live_count = live_index.shape[1]
    group_count = column_count // column_group
    normed_blocks = normed.reshape(tokens, column_count, block_size)

    def column_per_group(members):
        weight_part, index_part = members
        picked = jnp.take(normed_blocks, index_part.reshape(-1), axis=1).reshape(
            tokens, column_group, wide
        )
        return jnp.einsum("tjk,jbk->tjb", picked, weight_part, preferred_element_type=jnp.float32)

    result = lax.map(
        column_per_group,
        (
            section_weights.reshape(group_count, column_group, block_size, wide),
            live_index.reshape(group_count, column_group, live_count),
        ),
    )
    return result.transpose(1, 0, 2, 3).reshape(tokens, features)


def dense_transposed(section_weights, live_index):
    column_count, block_size, wide = section_weights.shape
    live_count = live_index.shape[1]
    group_count = column_count // column_group
    features = column_count * block_size
    targets = jnp.arange(column_count, dtype=jnp.int32)

    def dense_per_group(members):
        weight_part, index_part = members
        chosen = (index_part[:, :, None] == targets[None, None, :]).astype(jnp.bfloat16)
        slab = jnp.einsum(
            "jkr,jbka->jbra",
            chosen,
            weight_part.reshape(column_group, block_size, live_count, block_size),
            preferred_element_type=jnp.float32,
        )
        return slab.astype(jnp.bfloat16).reshape(column_group * block_size, features)

    slabs = lax.map(
        dense_per_group,
        (
            section_weights.reshape(group_count, column_group, block_size, wide),
            live_index.reshape(group_count, column_group, live_count),
        ),
    )
    return slabs.reshape(features, features)


def layer_forward(entering, section_weights, live_index):
    as_float = entering.astype(jnp.float32)
    inverse_rms = lax.rsqrt(jnp.mean(as_float * as_float, axis=-1, keepdims=True) + 1e-05)
    normed = (as_float * inverse_rms).astype(jnp.bfloat16)
    pre_act = column_products(normed, section_weights, live_index)
    return ((as_float + jax.nn.silu(pre_act)).astype(jnp.bfloat16), normed, pre_act)


def layer_backward(arriving, entering, pre_act, dense_weights):
    as_float = entering.astype(jnp.float32)
    inverse_rms = lax.rsqrt(jnp.mean(as_float * as_float, axis=-1, keepdims=True) + 1e-05)
    sigmoid_z = jax.nn.sigmoid(pre_act)
    grad_pre = (
        arriving.astype(jnp.float32) * (sigmoid_z * (1.0 + pre_act * (1.0 - sigmoid_z)))
    ).astype(jnp.bfloat16)
    grad_normed = jnp.dot(grad_pre, dense_weights, preferred_element_type=jnp.float32)
    scaled = as_float * inverse_rms
    leaving = (
        arriving.astype(jnp.float32)
        + inverse_rms
        * (grad_normed - scaled * jnp.mean(grad_normed * scaled, axis=-1, keepdims=True))
    ).astype(jnp.bfloat16)
    return (leaving, grad_pre)


def local(x_in, cotangent, weights, live_rows, moment, second):
    sections = lax.axis_size("pipe")
    section_index = lax.axis_index("pipe")
    micro_count, tokens, features = x_in.shape
    column_count = live_rows.shape[1]
    live_count = live_rows.shape[2]
    own_columns = weights.shape[1]
    block_size = weights.shape[2]
    live_index = live_rows[0]
    section_weights = lax.all_gather(weights[0], "dp", axis=0, tiled=True)
    tick_count = micro_count + sections - 1
    incoming = jnp.zeros((tokens, features), jnp.bfloat16)
    saved_in = jnp.zeros((micro_count, tokens, features), jnp.bfloat16)
    saved_normed = jnp.zeros((micro_count, tokens, features), jnp.bfloat16)
    saved_pre = jnp.zeros((micro_count, tokens, features), jnp.float32)
    for tick_index in range(tick_count):
        slot_raw = tick_index - section_index
        active_now = (slot_raw >= 0) & (slot_raw < micro_count)
        slot_index = jnp.clip(slot_raw, 0, micro_count - 1)
        entering = jnp.where(section_index == 0, x_in[min(tick_index, micro_count - 1)], incoming)

        def forward_work(state, slot_index=slot_index):
            current, store_in, store_normed, store_pre = state
            outgoing, normed, pre_act = layer_forward(current, section_weights, live_index)
            return (
                outgoing,
                store_in.at[slot_index].set(current),
                store_normed.at[slot_index].set(normed),
                store_pre.at[slot_index].set(pre_act),
            )

        def forward_skip(state):
            current, store_in, store_normed, store_pre = state
            return (jnp.zeros_like(current), store_in, store_normed, store_pre)

        outgoing, saved_in, saved_normed, saved_pre = lax.cond(
            active_now, forward_work, forward_skip, (entering, saved_in, saved_normed, saved_pre)
        )
        if tick_index + 1 < tick_count:
            incoming = shifted(outgoing, "pipe", 1)
    dense_weights = dense_transposed(section_weights, live_index)
    incoming_grad = jnp.zeros((tokens, features), jnp.bfloat16)
    saved_grad = jnp.zeros((micro_count, tokens, features), jnp.bfloat16)
    for tick_index in range(tick_count):
        slot_raw = tick_index - (sections - 1 - section_index)
        active_now = (slot_raw >= 0) & (slot_raw < micro_count)
        slot_index = jnp.clip(slot_raw, 0, micro_count - 1)
        arriving = jnp.where(
            section_index == sections - 1,
            cotangent[min(tick_index, micro_count - 1)],
            incoming_grad,
        )

        def backward_work(state, slot_index=slot_index):
            current, store_grad = state
            leaving, grad_pre = layer_backward(
                current, saved_in[slot_index], saved_pre[slot_index], dense_weights
            )
            return (leaving, store_grad.at[slot_index].set(grad_pre))

        def backward_skip(state):
            current, store_grad = state
            return (jnp.zeros_like(current), store_grad)

        leaving, saved_grad = lax.cond(
            active_now, backward_work, backward_skip, (arriving, saved_grad)
        )
        if tick_index + 1 < tick_count:
            incoming_grad = shifted(leaving, "pipe", -1)
    all_rows = micro_count * tokens
    normed_blocks = saved_normed.reshape(all_rows, column_count, block_size)
    grad_blocks = saved_grad.reshape(all_rows, column_count, block_size)
    inverse_tokens = 1.0 / (all_rows * lax.axis_size("dp"))
    cast_type = jnp.bfloat16
    group_size = math.gcd(column_count, column_group)
    group_count = column_count // group_size
    index_part = live_index.reshape(group_count, group_size, live_count)
    grad_part = grad_blocks.reshape(all_rows, group_count, group_size, block_size).transpose(
        1, 0, 2, 3
    )

    def grad_per_group(members):
        index_group, grad_group = members
        picked = jnp.take(normed_blocks, index_group.reshape(-1), axis=1).reshape(
            all_rows, group_size, live_count * block_size
        )
        return (
            jnp.einsum("tjk,tjb->jbk", picked, grad_group, preferred_element_type=jnp.float32)
            * inverse_tokens
        ).astype(cast_type)

    gradient = lax.psum_scatter(
        lax.map(grad_per_group, (index_part, grad_part)).reshape(
            column_count, block_size, live_count * block_size
        ),
        "dp",
        scatter_dimension=0,
        tiled=True,
    ).astype(jnp.float32)
    rate = 0.1 / math.sqrt(live_count * block_size)
    moment_new = 0.9 * moment[0] + 0.1 * gradient
    second_new = 0.95 * second[0] + 0.05 * gradient * gradient
    stepped = weights[0].astype(jnp.float32) - rate * moment_new / (jnp.sqrt(second_new) + 1e-08)
    own_index = lax.dynamic_slice_in_dim(
        live_index, lax.axis_index("dp") * own_columns, own_columns, 0
    )
    blocked = stepped.reshape(own_columns, block_size, live_count, block_size)
    magnitude = jnp.sqrt(jnp.sum(blocked * blocked, axis=(1, 3)))
    leafed = (
        blocked * shrink(magnitude, 0.15 * math.sqrt(block_size / live_count))[:, None, :, None]
    )
    block_squares = jnp.sum(leafed * leafed, axis=(1, 3))
    head_count = features // HEAD
    head_index = own_index // (HEAD // block_size)
    onehot = (
        head_index[:, :, None] == jnp.arange(head_count, dtype=jnp.int32)[None, None, :]
    ).astype(jnp.float32)
    head_squares = lax.psum(jnp.sum(onehot * block_squares[:, :, None], axis=(0, 1)), "dp")
    head_factor = shrink(jnp.sqrt(head_squares), 0.45 * math.sqrt(HEAD))
    headed = leafed * jnp.sum(onehot * head_factor[None, None, :], axis=2)[:, None, :, None]
    layer_squares = lax.psum(jnp.sum(headed * headed), "dp")
    layer_factor = shrink(jnp.sqrt(layer_squares), 0.45 * math.sqrt(features))
    weights_out = (
        (headed * layer_factor)
        .astype(jnp.bfloat16)
        .reshape(own_columns, block_size, live_count * block_size)
    )
    return (weights_out[None], moment_new[None], second_new[None])


def solution(mesh):
    placed = (
        P(None, "dp", None),
        P(None, "dp", None),
        P("pipe", "dp", None, None),
        P("pipe", None, None),
        P("pipe", "dp", None, None),
        P("pipe", "dp", None, None),
    )
    return jax.shard_map(
        local,
        mesh=mesh,
        in_specs=placed,
        out_specs=(
            P("pipe", "dp", None, None),
            P("pipe", "dp", None, None),
            P("pipe", "dp", None, None),
        ),
        check_vma=False,
    )
```

profile of v0, /device:TPU:1, one launch (start us, length us, event | category | flops | bytes accessed | tf_op | source)
XLA Modules:
  0.0 1587.1 jit_solution(2375558503213230283)
XLA Ops:
  8.0 78.6 %all-gather.3.cloned.1.call-done = bf16[1,64,64,2048]{3,2,0,1:T(8,128)(2,1)} async-done(((bf16[1,2,64,2048]{3,2,0,1:T(8,128)(2,1)}), bf16[1,64,64,2048]{3,2,0,1:T(8,128)(2,1)}) %all-gather.3.cloned.1.call-update) | async-done | bytes 16777232 | tf_op jit(solution)/shard_map/all_gather | solution.py:107
  87.3 84.7 %conditional.14 = (bf16[32,4096]{1,0:T(8,128)(2,1)S(1)}, bf16[4,32,4096]{2,1,0:T(8,128)(2,1)}, bf16[4,32,4096]{2,1,0:T(8,128)(2,1)}, f32[4,32,4096]{2,1,0:T(8,128)}) conditional(s32[]{:T(128)} %convert_element_type.242, () %tuple.272, (bf16[4,32,4096]{2,1,0:T(8,128)(2,1)}, pred[32,4096]{1,0:T(8,128)(4,1)S(1)}, bf16[32,4096]{1,0:T(8,128)(2,1)S(1)}, ...), branch_computations={%region_0.1_spmd, %region_1.7_spmd} | conditional | flops 69864752 | bytes 28641040 | solution.py:133
  95.7 69.9 %while.112 = (s32[]{:T(128)}, f32[8,32,8,64]{3,1,2,0:T(8,128)}, bf16[8,8,64,2048]{3,2,1,0:T(8,128)(2,1)}, s32[8,8,32]{2,1,0:T(8,128)S(1)}, bf16[32,64,64]{2,0,1:T(8,128)(2,1)S(1)}, /*index=5*/s32[]{:T(128)}) while((s32[]{:T(128)}, f32[8,32,8,64]{3,1,2,0:T(8,128)}, bf16[8,8,64,2048]{3,2,1,0:T(8,128)(2,1)}, s32[8,8,32]{2,1,0:T(8,128)S(1)}, ...), condition=%wide.region_4.5_spmd, body=%wide.region_3.4_spmd.sunk | while | flops 67636480 | bytes 11680329 | solution.py:35
  174.0 6.0 collective-permute-done
  180.1 83.5 %conditional.15 = (bf16[32,4096]{1,0:T(8,128)(2,1)}, bf16[4,32,4096]{2,1,0:T(8,128)(2,1)}, bf16[4,32,4096]{2,1,0:T(8,128)(2,1)}, f32[4,32,4096]{2,1,0:T(8,128)}) conditional(s32[]{:T(128)} %convert_element_type.241, (bf16[4,32,4096]{2,1,0:T(8,128)(2,1)}, bf16[4,32,4096]{2,1,0:T(8,128)(2,1)}, f32[4,32,4096]{2,1,0:T(8,128)}) %tuple.274, ...), branch_computations={%region_6.8_spmd, %region_7.13_spmd} | conditional | flops 69864752 | bytes 21301482 | solution.py:133
  187.9 69.8 %while.113 = (s32[]{:T(128)}, f32[8,32,8,64]{3,1,2,0:T(8,128)}, bf16[8,8,64,2048]{3,2,1,0:T(8,128)(2,1)}, s32[8,8,32]{2,1,0:T(8,128)S(1)}, bf16[32,64,64]{2,0,1:T(8,128)(2,1)S(1)}, /*index=5*/s32[]{:T(128)}) while((s32[]{:T(128)}, f32[8,32,8,64]{3,1,2,0:T(8,128)}, bf16[8,8,64,2048]{3,2,1,0:T(8,128)(2,1)}, s32[8,8,32]{2,1,0:T(8,128)S(1)}, ...), condition=%wide.region_10.11_spmd, body=%wide.region_9.10_spmd.sunk | while | flops 67636480 | bytes 11680329 | solution.py:35
  272.8 83.2 %conditional.16 = (bf16[32,4096]{1,0:T(8,128)(2,1)}, bf16[4,32,4096]{2,1,0:T(8,128)(2,1)}, bf16[4,32,4096]{2,1,0:T(8,128)(2,1)}, f32[4,32,4096]{2,1,0:T(8,128)}) conditional(s32[]{:T(128)} %convert_element_type.240, (bf16[4,32,4096]{2,1,0:T(8,128)(2,1)}, bf16[4,32,4096]{2,1,0:T(8,128)(2,1)}, f32[4,32,4096]{2,1,0:T(8,128)}) %tuple.276, ...), branch_computations={%region_12.14_spmd, %region_13.19_spmd} | conditional | flops 69864752 | bytes 21301482 | solution.py:133
  280.3 69.8 %while.114 = (s32[]{:T(128)}, f32[8,32,8,64]{3,1,2,0:T(8,128)}, bf16[8,8,64,2048]{3,2,1,0:T(8,128)(2,1)}, s32[8,8,32]{2,1,0:T(8,128)S(1)}, bf16[32,64,64]{2,0,1:T(8,128)(2,1)S(1)}, /*index=5*/s32[]{:T(128)}) while((s32[]{:T(128)}, f32[8,32,8,64]{3,1,2,0:T(8,128)}, bf16[8,8,64,2048]{3,2,1,0:T(8,128)(2,1)}, s32[8,8,32]{2,1,0:T(8,128)S(1)}, ...), condition=%wide.region_16.17_spmd, body=%wide.region_15.16_spmd.sunk | while | flops 67636480 | bytes 11680329 | solution.py:35
  364.2 83.4 %conditional.17 = (bf16[32,4096]{1,0:T(8,128)(2,1)}, bf16[4,32,4096]{2,1,0:T(8,128)(2,1)}, bf16[4,32,4096]{2,1,0:T(8,128)(2,1)}, f32[4,32,4096]{2,1,0:T(8,128)}) conditional(s32[]{:T(128)} %convert_element_type.239, (bf16[4,32,4096]{2,1,0:T(8,128)(2,1)}, bf16[4,32,4096]{2,1,0:T(8,128)(2,1)}, f32[4,32,4096]{2,1,0:T(8,128)}) %tuple.278, ...), branch_computations={%region_18.20_spmd, %region_19.25_spmd} | conditional | flops 69864752 | bytes 21301482 | solution.py:133
  371.8 69.8 %while.115 = (s32[]{:T(128)}, f32[8,32,8,64]{3,1,2,0:T(8,128)}, bf16[8,8,64,2048]{3,2,1,0:T(8,128)(2,1)}, s32[8,8,32]{2,1,0:T(8,128)S(1)}, bf16[32,64,64]{2,0,1:T(8,128)(2,1)S(1)}, /*index=5*/s32[]{:T(128)}) while((s32[]{:T(128)}, f32[8,32,8,64]{3,1,2,0:T(8,128)}, bf16[8,8,64,2048]{3,2,1,0:T(8,128)(2,1)}, s32[8,8,32]{2,1,0:T(8,128)S(1)}, ...), condition=%wide.region_22.23_spmd, body=%wide.region_21.22_spmd.sunk | while | flops 67636480 | bytes 11680329 | solution.py:35
  456.2 85.9 %collective-permute-start.4 = (bf16[32,4096]{1,0:T(8,128)(2,1)}, bf16[32,4096]{1,0:T(8,128)(2,1)S(1)}, u32[]{:S(2)}, u32[]{:S(2)}) collective-permute-start(bf16[32,4096]{1,0:T(8,128)(2,1)} %get-tuple-element.1129), channel_id=1, source_target_pairs={{0,32},{32,64},{64,96},{1,33},{33,65},{65,97},{2,34},{34,66},{66,9... | collective-permute-start | bytes 786440 | tf_op jit(solution)/shard_map/ppermute | solution.py:14
  546.9 8.3 collective-permute-start.5
  555.2 356.7 %while.120 = (s32[]{:T(128)}, bf16[8,512,4096]{2,1,0:T(8,128)(2,1)}, bf16[8,8,64,2048]{3,2,1,0:T(8,128)(2,1)}, s32[8,8,32]{2,1,0:T(8,128)}, s32[]{:T(128)}) while((s32[]{:T(128)}, bf16[8,512,4096]{2,1,0:T(8,128)(2,1)}, bf16[8,8,64,2048]{3,2,1,0:T(8,128)(2,1)}, s32[8,8,32]{2,1,0:T(8,128)}, s32[]{:T(128)}) %tuple.546), condition=%wide.region_43.45_spmd.clone, body=%wide.region_42.44_spmd.clone.sunk | while | flops 136331264 | bytes 39849540 | solution.py:63
  556.9 5.3 reshape.1425
  562.9 8.2 convert_bitcast_fusion.2
  571.2 11.9 copy.214
  583.1 12.0 broadcast_in_dim.172
  601.5 5.3 reshape.1425
  607.5 8.2 convert_bitcast_fusion.2
  615.7 11.9 copy.214
  627.7 12.0 broadcast_in_dim.172
  646.1 5.3 reshape.1425
  652.1 8.2 convert_bitcast_fusion.2
  660.3 11.9 copy.214
  672.3 12.0 broadcast_in_dim.172
  696.7 8.2 convert_bitcast_fusion.2
  704.9 11.9 copy.214
  716.9 12.0 broadcast_in_dim.172
  741.3 8.2 convert_bitcast_fusion.2
  749.5 11.9 copy.214
  761.4 12.0 broadcast_in_dim.172
  785.8 8.2 convert_bitcast_fusion.2
  794.0 11.9 copy.214
  806.0 12.0 broadcast_in_dim.172
  824.4 5.3 reshape.1425
  830.4 8.2 convert_bitcast_fusion.2
  838.6 11.9 copy.214
  850.6 12.0 broadcast_in_dim.172
  875.0 8.2 convert_bitcast_fusion.2
  883.2 11.9 copy.214
  895.2 12.0 broadcast_in_dim.172
  915.5 83.3 %collective-permute-done.6 = bf16[32,4096]{1,0:T(8,128)(2,1)S(1)} collective-permute-done((bf16[32,4096]{1,0:T(8,128)(2,1)S(1)}, bf16[32,4096]{1,0:T(8,128)(2,1)S(1)}, u32[]{:S(2)}, u32[]{:S(2)}) %collective-permute-start.6) | collective-permute-done | bytes 262176 | tf_op jit(solution)/shard_map/ppermute | solution.py:14
  1000.1 6.2 collective-permute-done.7
  1009.1 140.8 %collective-permute-done.8 = bf16[32,4096]{1,0:T(8,128)(2,1)S(1)} collective-permute-done((bf16[32,4096]{1,0:T(8,128)(2,1)S(1)}, bf16[32,4096]{1,0:T(8,128)(2,1)S(1)}, u32[]{:S(2)}, u32[]{:S(2)}) %collective-permute-start.8) | collective-permute-done | bytes 262176 | tf_op jit(solution)/shard_map/ppermute | solution.py:14
  1149.9 20.3 %conditional.24 = (bf16[32,4096]{1,0:T(8,128)(2,1)S(1)}, bf16[4,32,4096]{2,1,0:T(8,128)(2,1)}) conditional(s32[]{:T(128)} %convert_element_type.232, bf16[4,32,4096]{2,1,0:T(8,128)(2,1)} %get-tuple-element.1141, (pred[32,4096]{1,0:T(8,128)(4,1)S(1)}, bf16[32,4096]{1,0:T(8,128)(2,1)S(1)}, bf16[32,4096]{1,0:T(8,128)(2,1)S(1)}, s32[]{:T(128)}, ...), branch_computations={%region_59.61_spmd, %region_60.65_spmd} | conditional | flops 1077411840 | bytes 38537416 | solution.py:162
  1155.1 13.9 fusion.45
  1171.5 5.8 collective-permute-done.9
  1177.3 20.3 %conditional.25 = (bf16[32,4096]{1,0:T(8,128)(2,1)S(1)}, bf16[4,32,4096]{2,1,0:T(8,128)(2,1)}) conditional(s32[]{:T(128)} %convert_element_type.231, bf16[4,32,4096]{2,1,0:T(8,128)(2,1)} %get-tuple-element.1143, (pred[32,4096]{1,0:T(8,128)(4,1)S(1)}, bf16[32,4096]{1,0:T(8,128)(2,1)S(1)}, bf16[32,4096]{1,0:T(8,128)(2,1)S(1)}, s32[]{:T(128)}, ...), branch_computations={%region_64.66_spmd, %region_65.70_spmd} | conditional | flops 1077411840 | bytes 38537416 | solution.py:162
  1182.5 13.9 fusion.59
  1198.9 5.8 collective-permute-done.10
  1204.7 21.0 %conditional.26 = (bf16[32,4096]{1,0:T(8,128)(2,1)}, bf16[4,32,4096]{2,1,0:T(8,128)(2,1)}) conditional(s32[]{:T(128)} %convert_element_type.230, bf16[4,32,4096]{2,1,0:T(8,128)(2,1)} %get-tuple-element.1145, (pred[32,4096]{1,0:T(8,128)(4,1)S(1)}, bf16[32,4096]{1,0:T(8,128)(2,1)S(1)}, bf16[32,4096]{1,0:T(8,128)(2,1)S(1)}, s32[]{:T(128)}, ...), branch_computations={%region_69.71_spmd, %region_70.75_spmd} | conditional | flops 1077411840 | bytes 38537416 | solution.py:162
  1209.9 13.9 fusion.73
  1243.5 80.6 %while.119 = (s32[]{:T(128)}, bf16[8,8,64,2048]{3,2,1,0:T(8,128)(2,1)}, bf16[8,128,8,64]{1,3,2,0:T(8,128)(2,1)}, s32[8,8,32]{2,1,0:T(8,128)}, bf16[128,64,64]{0,2,1:T(8,128)(2,1)S(1)}, /*index=5*/s32[]{:T(128)}) while((s32[]{:T(128)}, bf16[8,8,64,2048]{3,2,1,0:T(8,128)(2,1)}, bf16[8,128,8,64]{1,3,2,0:T(8,128)(2,1)}, ...), condition=%wide.region_78.80_spmd, body=%wide.region_77.79_spmd.sunk | while | flops 272633088 | bytes 14890569 | solution.py:190
  1247.6 6.1 fusion.280
  1257.7 6.1 fusion.280
  1267.7 6.1 fusion.280
  1277.8 6.1 fusion.280
  1287.9 6.0 fusion.280
  1298.0 6.1 fusion.280
  1308.1 6.0 fusion.280
  1318.1 6.0 fusion.280
  1324.4 120.4 %reduce-scatter.2.cloned.1.call-done = bf16[2,64,2048]{2,1,0:T(8,128)(2,1)} async-done(((bf16[64,64,2048]{2,1,0:T(8,128)(2,1)}), bf16[2,64,2048]{2,1,0:T(8,128)(2,1)}) %reduce-scatter.2.cloned.1.call-update) | async-done | bytes 524304 | tf_op jit(solution)/shard_map/reduce_scatter | solution.py:189
  1449.1 63.9 %psum.14 = f32[32]{0:T(128)S(1)} all-reduce(f32[32]{0:T(128)S(1)} %select_reduce_fusion.1), channel_id=1, replica_groups=mesh['pipe'=4,'dp'=32] {'dp'}, use_global_device_ids=true, to_apply=%region_85.87 | all-reduce | flops 32 | bytes 256 | tf_op jit(solution)/shard_map/psum | solution.py:215
  1514.2 64.2 %psum.15 = f32[]{:T(128)} all-reduce(f32[]{:T(128)} %multiply_reduce_fusion), channel_id=1, replica_groups=mesh['pipe'=4,'dp'=32] {'dp'}, use_global_device_ids=true, to_apply=%region_88.90 | all-reduce | flops 1 | bytes 8 | tf_op jit(solution)/shard_map/psum | solution.py:218
  (571 shorter events, 538.1 us)
Async XLA Ops:
  7.2 79.4 %all-gather.3.cloned.1.call-start = ((), (), s32[]{:S(2)}) async-start(), calls=%async_computation.2 | async-start | bytes 17301504 | tf_op jit(solution)/shard_map/all_gather | solution.py:107
  7.9 1436.9 %reduce-scatter.2.cloned.1.call-start = ((), (), s32[]{:S(2)}) async-start(), calls=%async_computation.1 | async-start | bytes 17301504 | tf_op jit(solution)/shard_map/reduce_scatter | solution.py:189
  86.6 0.7 copy-start.1
  92.1 3.6 copy-start.5
  168.1 2.8 copy-start
  172.0 0.7 copy-start.11
  172.7 7.4 collective-permute-start
  181.9 5.9 copy-start.6
  263.6 9.2 collective-permute-start.1
  274.3 5.9 copy-start.7
  355.9 8.3 collective-permute-start.2
  365.7 6.1 copy-start.8
  447.6 7.6 collective-permute-start.3
  455.2 90.5 %copy-start.4 = (s32[1,64,32]{1,2,0:T(8,128)S(1)}, s32[1,64,32]{1,2,0:T(8,128)}, u32[]{:S(2)}) copy-start(s32[1,64,32]{1,2,0:T(8,128)} %param.113) | copy-start | bytes 24580
  456.2 89.5 %collective-permute-start.4 = (bf16[32,4096]{1,0:T(8,128)(2,1)}, bf16[32,4096]{1,0:T(8,128)(2,1)S(1)}, u32[]{:S(2)}, u32[]{:S(2)}) collective-permute-start(bf16[32,4096]{1,0:T(8,128)(2,1)} %get-tuple-element.1129), channel_id=1, source_target_pairs={{0,32},{32,64},{64,96},{1,33},{33,65},{65,97},{2,34},{34,66},{66,9... | collective-permute-start | bytes 786440 | tf_op jit(solution)/shard_map/ppermute | solution.py:14
  546.9 365.0 %collective-permute-start.5 = (bf16[32,4096]{1,0:T(8,128)(2,1)}, bf16[32,4096]{1,0:T(8,128)(2,1)S(1)}, u32[]{:S(2)}, u32[]{:S(2)}) collective-permute-start(bf16[32,4096]{1,0:T(8,128)(2,1)} %get-tuple-element.1133), channel_id=1, source_target_pairs={{0,32},{32,64},{64,96},{1,33},{33,65},{65,97},{2,34},{34,66},{66,9... | collective-permute-start | bytes 786440 | tf_op jit(solution)/shard_map/ppermute | solution.py:14
  911.9 1.0 copy-start.2
  914.1 84.6 %collective-permute-start.6 = (bf16[32,4096]{1,0:T(8,128)(2,1)S(1)}, bf16[32,4096]{1,0:T(8,128)(2,1)S(1)}, u32[]{:S(2)}, u32[]{:S(2)}) collective-permute-start(bf16[32,4096]{1,0:T(8,128)(2,1)S(1)} %get-tuple-element.1138), channel_id=1, source_target_pairs={{32,0},{64,32},{96,64},{33,1},{65,33},{97,65},{34,2},{66,34},{98,6... | collective-permute-start | bytes 786440 | tf_op jit(solution)/shard_map/ppermute | solution.py:14
  998.8 7.5 collective-permute-start.7
  1006.4 143.5 %collective-permute-start.8 = (bf16[32,4096]{1,0:T(8,128)(2,1)S(1)}, bf16[32,4096]{1,0:T(8,128)(2,1)S(1)}, u32[]{:S(2)}, u32[]{:S(2)}) collective-permute-start(bf16[32,4096]{1,0:T(8,128)(2,1)S(1)} %get-tuple-element.1142), channel_id=1, source_target_pairs={{32,0},{64,32},{96,64},{33,1},{65,33},{97,65},{34,2},{66,34},{98,6... | collective-permute-start | bytes 786440 | tf_op jit(solution)/shard_map/ppermute | solution.py:14
  1170.2 7.1 collective-permute-start.9
  1197.6 7.1 collective-permute-start.10
  1225.7 7.4 collective-permute-start.11
  1324.2 120.6 %copy-start.3 = (bf16[1,2,64,2048]{3,2,1,0:T(8,128)(2,1)S(1)}, bf16[1,2,64,2048]{3,2,1,0:T(8,128)(2,1)}, u32[]{:S(2)}) copy-start(bf16[1,2,64,2048]{3,2,1,0:T(8,128)(2,1)} %param.112) | copy-start | bytes 1572868
  1324.2 120.6 %copy-start.10 = (f32[1,2,64,2048]{3,2,1,0:T(8,128)S(1)}, f32[1,2,64,2048]{3,2,1,0:T(8,128)}, u32[]{:S(2)}) copy-start(f32[1,2,64,2048]{3,2,1,0:T(8,128)} %param.115) | copy-start | bytes 3145732
Sparse Core Ops, SparseCore 0:
  10.3 76.2 all-gather.2
  1324.3 120.4 reduce-scatter.1
where the time goes:
time: 1600 us; the launch traced here: 1590 us
  local copies, waits for them, and re-layouts  494 us (31%)
  waiting for transfers between devices  462 us (29%)
  matrix products  265 us (17%)
  blocking collectives  128 us (8%)
  starting transfers between devices  116 us (7%)
  other arithmetic  103 us (6%)
    ppermute x12, waiting for transfers between devices, shifted(): lax.ppermute(value, axis, [(source, source + steps) for source in range(l...  262 us
    reduce_scatter x1, waiting for transfers between devices, local(): lax.psum_scatter(lax.map(grad_per_group, (index_part, grad_part)).reshape...  120 us
    ppermute x12, starting transfers between devices, shifted(): lax.ppermute(value, axis, [(source, source + steps) for source in range(l...  116 us
    dot_general x32, matrix products, column_per_group(): jnp.einsum('tjk,jbk->tjb', picked, weight_part, preferred_element_type=jn...  110 us
    broadcast_in_dim x8, local copies, waits for them, and re-layouts, dense_transposed(): lax.map(dense_per_group, (section_weights.reshape(group_count, column_gro...  96.3 us
    convert_element_type x8, local copies, waits for them, and re-layouts, dense_per_group(): slab.astype(jnp.bfloat16).reshape(column_group * block_size, features)  95.6 us
    all_gather x1, waiting for transfers between devices, local(): section_weights = lax.all_gather(weights[0], 'dp', axis=0, tiled=True)  78.6 us
    reshape x32, local copies, waits for them, and re-layouts, column_per_group(): jnp.take(normed_blocks, index_part.reshape(-1), axis=1)  78 us
  transfers between devices with their start and end apart: 14, of which 13 were waited for; matrix products, arithmetic and copies ran while one was open for 23% of the time, Pallas kernels for 0%

commit v1 on v0

--- a/solution.py
+++ b/solution.py
@@ -6,6 +6,11 @@
 
 HEAD = 128
 column_group = 8
+
+
+def swapped_in(value, axis, d):
+    repeated = jnp.stack([value] * lax.axis_size(axis))
+    return jnp.concatenate(lax.all_to_all(repeated, axis, 0, 0), axis=d)
 
 
 def shifted(value, axis, steps):
@@ -104,7 +109,7 @@
     own_columns = weights.shape[1]
     block_size = weights.shape[2]
     live_index = live_rows[0]
-    section_weights = lax.all_gather(weights[0], "dp", axis=0, tiled=True)
+    section_weights = swapped_in(weights[0], "dp", 0)
     tick_count = micro_count + sections - 1
     incoming = jnp.zeros((tokens, features), jnp.bfloat16)
     saved_in = jnp.zeros((micro_count, tokens, features), jnp.bfloat16)

time: 1600 us -> 1750 us (1.094)
  waiting for transfers between devices: 462 us -> 592 us
    all_to_all x0 -> x1, waiting for transfers between devices: none -> 202 us  [swapped_in(): return jnp.concatenate(lax.all_to_all(repeated, axis, 0, 0), axis=d)]
    all_gather x1 -> x0, waiting for transfers between devices: 78.6 us -> none  [local(): section_weights = lax.all_gather(weights[0], 'dp', axis=0, tiled=True)]
  transfers between devices with their start and end apart: 14 -> 14, of which waited for: 13 -> 13; matrix products, arithmetic and copies ran while one was open for 23% -> 21% of each run, Pallas kernels for 0% -> 0%
where the time goes in v1:
time: 1750 us; the launch traced here: 1730 us
  waiting for transfers between devices  592 us (34%)
  local copies, waits for them, and re-layouts  500 us (29%)
  matrix products  265 us (15%)
  blocking collectives  128 us (7%)
  starting transfers between devices  125 us (7%)
  other arithmetic  103 us (6%)
    ppermute x12, waiting for transfers between devices, shifted(): lax.ppermute(value, axis, [(source, source + steps) for source in range(l...  257 us
    all_to_all x1, waiting for transfers between devices, swapped_in(): return jnp.concatenate(lax.all_to_all(repeated, axis, 0, 0), axis=d)  202 us
    reduce_scatter x1, waiting for transfers between devices, local(): lax.psum_scatter(lax.map(grad_per_group, (index_part, grad_part)).reshape...  133 us
    ppermute x12, starting transfers between devices, shifted(): lax.ppermute(value, axis, [(source, source + steps) for source in range(l...  115 us
    dot_general x32, matrix products, column_per_group(): jnp.einsum('tjk,jbk->tjb', picked, weight_part, preferred_element_type=jn...  110 us
    broadcast_in_dim x8, local copies, waits for them, and re-layouts, dense_transposed(): lax.map(dense_per_group, (section_weights.reshape(group_count, column_gro...  96.3 us
    convert_element_type x8, local copies, waits for them, and re-layouts, dense_per_group(): slab.astype(jnp.bfloat16).reshape(column_group * block_size, features)  95.6 us
    reshape x32, local copies, waits for them, and re-layouts, column_per_group(): jnp.take(normed_blocks, index_part.reshape(-1), axis=1)  78 us
  transfers between devices with their start and end apart: 14, of which 13 were waited for; matrix products, arithmetic and copies ran while one was open for 21% of the time, Pallas kernels for 0%

profile of v1, /device:TPU:1, one launch (start us, length us, event | category | flops | bytes accessed | tf_op | source)
XLA Modules:
  0.0 1731.2 jit_solution(6647151823288985188)
XLA Ops:
  7.2 6.8 stack.3
  14.0 9.6 all-to-all-start
  23.7 201.9 %all-to-all-done = bf16[32,2,64,2048]{3,2,1,0:T(8,128)(2,1)} async-done(((bf16[32,2,64,2048]{3,2,1,0:T(8,128)(2,1)}), bf16[32,2,64,2048]{3,2,1,0:T(8,128)(2,1)}, u32[]{:S(2)}, u32[]{:S(2)}) %all-to-all-start) | async-done | bytes 16777248 | tf_op jit(solution)/shard_map/all_to_all | solution.py:13
  226.3 84.7 %conditional.14 = (bf16[32,4096]{1,0:T(8,128)(2,1)S(1)}, bf16[4,32,4096]{2,1,0:T(8,128)(2,1)}, bf16[4,32,4096]{2,1,0:T(8,128)(2,1)}, f32[4,32,4096]{2,1,0:T(8,128)}) conditional(s32[]{:T(128)} %convert_element_type.242, () %tuple.272, (bf16[4,32,4096]{2,1,0:T(8,128)(2,1)}, pred[32,4096]{1,0:T(8,128)(4,1)S(1)}, bf16[32,4096]{1,0:T(8,128)(2,1)S(1)}, ...), branch_computations={%region_0.1_spmd, %region_1.7_spmd} | conditional | flops 69864752 | bytes 28608244 | solution.py:138
  234.7 69.9 %while.112 = (s32[]{:T(128)}, f32[8,32,8,64]{3,1,2,0:T(8,128)}, bf16[8,8,64,2048]{3,2,1,0:T(8,128)(2,1)}, s32[8,8,32]{2,1,0:T(8,128)S(1)}, bf16[32,64,64]{2,0,1:T(8,128)(2,1)S(1)}, /*index=5*/s32[]{:T(128)}) while((s32[]{:T(128)}, f32[8,32,8,64]{3,1,2,0:T(8,128)}, bf16[8,8,64,2048]{3,2,1,0:T(8,128)(2,1)}, s32[8,8,32]{2,1,0:T(8,128)S(1)}, ...), condition=%wide.region_4.5_spmd, body=%wide.region_3.4_spmd.sunk | while | flops 67636480 | bytes 11680329 | solution.py:40
  316.6 83.5 %conditional.15 = (bf16[32,4096]{1,0:T(8,128)(2,1)}, bf16[4,32,4096]{2,1,0:T(8,128)(2,1)}, bf16[4,32,4096]{2,1,0:T(8,128)(2,1)}, f32[4,32,4096]{2,1,0:T(8,128)}) conditional(s32[]{:T(128)} %convert_element_type.241, (bf16[4,32,4096]{2,1,0:T(8,128)(2,1)}, bf16[4,32,4096]{2,1,0:T(8,128)(2,1)}, f32[4,32,4096]{2,1,0:T(8,128)}) %tuple.274, ...), branch_computations={%region_6.8_spmd, %region_7.13_spmd} | conditional | flops 69864752 | bytes 21268686 | solution.py:138
  324.4 69.8 %while.113 = (s32[]{:T(128)}, f32[8,32,8,64]{3,1,2,0:T(8,128)}, bf16[8,8,64,2048]{3,2,1,0:T(8,128)(2,1)}, s32[8,8,32]{2,1,0:T(8,128)S(1)}, bf16[32,64,64]{2,0,1:T(8,128)(2,1)S(1)}, /*index=5*/s32[]{:T(128)}) while((s32[]{:T(128)}, f32[8,32,8,64]{3,1,2,0:T(8,128)}, bf16[8,8,64,2048]{3,2,1,0:T(8,128)(2,1)}, s32[8,8,32]{2,1,0:T(8,128)S(1)}, ...), condition=%wide.region_10.11_spmd, body=%wide.region_9.10_spmd.sunk | while | flops 67636480 | bytes 11680329 | solution.py:40
  407.4 83.2 %conditional.16 = (bf16[32,4096]{1,0:T(8,128)(2,1)}, bf16[4,32,4096]{2,1,0:T(8,128)(2,1)}, bf16[4,32,4096]{2,1,0:T(8,128)(2,1)}, f32[4,32,4096]{2,1,0:T(8,128)}) conditional(s32[]{:T(128)} %convert_element_type.240, (bf16[4,32,4096]{2,1,0:T(8,128)(2,1)}, bf16[4,32,4096]{2,1,0:T(8,128)(2,1)}, f32[4,32,4096]{2,1,0:T(8,128)}) %tuple.276, ...), branch_computations={%region_12.14_spmd, %region_13.19_spmd} | conditional | flops 69864752 | bytes 21268686 | solution.py:138
  414.9 69.8 %while.114 = (s32[]{:T(128)}, f32[8,32,8,64]{3,1,2,0:T(8,128)}, bf16[8,8,64,2048]{3,2,1,0:T(8,128)(2,1)}, s32[8,8,32]{2,1,0:T(8,128)S(1)}, bf16[32,64,64]{2,0,1:T(8,128)(2,1)S(1)}, /*index=5*/s32[]{:T(128)}) while((s32[]{:T(128)}, f32[8,32,8,64]{3,1,2,0:T(8,128)}, bf16[8,8,64,2048]{3,2,1,0:T(8,128)(2,1)}, s32[8,8,32]{2,1,0:T(8,128)S(1)}, ...), condition=%wide.region_16.17_spmd, body=%wide.region_15.16_spmd.sunk | while | flops 67636480 | bytes 11680329 | solution.py:40
  497.9 83.4 %conditional.17 = (bf16[32,4096]{1,0:T(8,128)(2,1)}, bf16[4,32,4096]{2,1,0:T(8,128)(2,1)}, bf16[4,32,4096]{2,1,0:T(8,128)(2,1)}, f32[4,32,4096]{2,1,0:T(8,128)}) conditional(s32[]{:T(128)} %convert_element_type.239, (bf16[4,32,4096]{2,1,0:T(8,128)(2,1)}, bf16[4,32,4096]{2,1,0:T(8,128)(2,1)}, f32[4,32,4096]{2,1,0:T(8,128)}) %tuple.278, ...), branch_computations={%region_18.20_spmd, %region_19.25_spmd} | conditional | flops 69864752 | bytes 21268686 | solution.py:138
  505.5 69.8 %while.115 = (s32[]{:T(128)}, f32[8,32,8,64]{3,1,2,0:T(8,128)}, bf16[8,8,64,2048]{3,2,1,0:T(8,128)(2,1)}, s32[8,8,32]{2,1,0:T(8,128)S(1)}, bf16[32,64,64]{2,0,1:T(8,128)(2,1)S(1)}, /*index=5*/s32[]{:T(128)}) while((s32[]{:T(128)}, f32[8,32,8,64]{3,1,2,0:T(8,128)}, bf16[8,8,64,2048]{3,2,1,0:T(8,128)(2,1)}, s32[8,8,32]{2,1,0:T(8,128)S(1)}, ...), condition=%wide.region_22.23_spmd, body=%wide.region_21.22_spmd.sunk | while | flops 67636480 | bytes 11680329 | solution.py:40
  589.5 85.9 %collective-permute-start.4 = (bf16[32,4096]{1,0:T(8,128)(2,1)}, bf16[32,4096]{1,0:T(8,128)(2,1)S(1)}, u32[]{:S(2)}, u32[]{:S(2)}) collective-permute-start(bf16[32,4096]{1,0:T(8,128)(2,1)} %get-tuple-element.1129), channel_id=1, source_target_pairs={{0,32},{32,64},{64,96},{1,33},{33,65},{65,97},{2,34},{34,66},{66,9... | collective-permute-start | bytes 786440 | tf_op jit(solution)/shard_map/ppermute | solution.py:19
  680.2 8.3 collective-permute-start.5
  688.5 356.7 %while.120 = (s32[]{:T(128)}, bf16[8,512,4096]{2,1,0:T(8,128)(2,1)}, bf16[8,8,64,2048]{3,2,1,0:T(8,128)(2,1)}, s32[8,8,32]{2,1,0:T(8,128)}, s32[]{:T(128)}) while((s32[]{:T(128)}, bf16[8,512,4096]{2,1,0:T(8,128)(2,1)}, bf16[8,8,64,2048]{3,2,1,0:T(8,128)(2,1)}, s32[8,8,32]{2,1,0:T(8,128)}, s32[]{:T(128)}) %tuple.519), condition=%wide.region_43.45_spmd.clone, body=%wide.region_42.44_spmd.clone.sunk | while | flops 136331264 | bytes 39849540 | solution.py:68
  696.3 8.2 convert_bitcast_fusion.2
  704.5 11.9 copy.165
  716.4 12.0 broadcast_in_dim.172
  734.8 5.3 reshape.1398
  740.8 8.2 convert_bitcast_fusion.2
  749.0 11.9 copy.165
  761.0 12.0 broadcast_in_dim.172
  779.4 5.3 reshape.1398
  785.4 8.2 convert_bitcast_fusion.2
  793.6 11.9 copy.165
  805.6 12.0 broadcast_in_dim.172
  830.0 8.2 convert_bitcast_fusion.2
  838.2 11.9 copy.165
  850.2 12.0 broadcast_in_dim.172
  868.6 5.3 reshape.1398
  874.6 8.2 convert_bitcast_fusion.2
  882.8 11.9 copy.165
  894.8 12.0 broadcast_in_dim.172
  919.1 8.2 convert_bitcast_fusion.2
  927.3 11.9 copy.165
  939.3 12.0 broadcast_in_dim.172
  963.7 8.2 convert_bitcast_fusion.2
  971.9 11.9 copy.165
  983.9 12.0 broadcast_in_dim.172
  1008.3 8.2 convert_bitcast_fusion.2
  1016.6 11.9 copy.165
  1028.5 12.0 broadcast_in_dim.172
  1048.8 82.4 %collective-permute-done.6 = bf16[32,4096]{1,0:T(8,128)(2,1)S(1)} collective-permute-done((bf16[32,4096]{1,0:T(8,128)(2,1)S(1)}, bf16[32,4096]{1,0:T(8,128)(2,1)S(1)}, u32[]{:S(2)}, u32[]{:S(2)}) %collective-permute-start.6) | collective-permute-done | bytes 262176 | tf_op jit(solution)/shard_map/ppermute | solution.py:19
  1132.5 5.8 collective-permute-done.7
  1141.0 140.7 %collective-permute-done.8 = bf16[32,4096]{1,0:T(8,128)(2,1)S(1)} collective-permute-done((bf16[32,4096]{1,0:T(8,128)(2,1)S(1)}, bf16[32,4096]{1,0:T(8,128)(2,1)S(1)}, u32[]{:S(2)}, u32[]{:S(2)}) %collective-permute-start.8) | collective-permute-done | bytes 262176 | tf_op jit(solution)/shard_map/ppermute | solution.py:19
  1281.7 20.3 %conditional.24 = (bf16[32,4096]{1,0:T(8,128)(2,1)S(1)}, bf16[4,32,4096]{2,1,0:T(8,128)(2,1)}) conditional(s32[]{:T(128)} %convert_element_type.232, bf16[4,32,4096]{2,1,0:T(8,128)(2,1)} %get-tuple-element.1141, (pred[32,4096]{1,0:T(8,128)(4,1)S(1)}, bf16[32,4096]{1,0:T(8,128)(2,1)S(1)}, bf16[32,4096]{1,0:T(8,128)(2,1)S(1)}, s32[]{:T(128)}, ...), branch_computations={%region_59.61_spmd, %region_60.65_spmd} | conditional | flops 1077411840 | bytes 38537416 | solution.py:167
  1286.9 13.9 fusion.45
  1303.3 5.8 collective-permute-done.9
  1309.1 20.3 %conditional.25 = (bf16[32,4096]{1,0:T(8,128)(2,1)S(1)}, bf16[4,32,4096]{2,1,0:T(8,128)(2,1)}) conditional(s32[]{:T(128)} %convert_element_type.231, bf16[4,32,4096]{2,1,0:T(8,128)(2,1)} %get-tuple-element.1143, (pred[32,4096]{1,0:T(8,128)(4,1)S(1)}, bf16[32,4096]{1,0:T(8,128)(2,1)S(1)}, bf16[32,4096]{1,0:T(8,128)(2,1)S(1)}, s32[]{:T(128)}, ...), branch_computations={%region_64.66_spmd, %region_65.70_spmd} | conditional | flops 1077411840 | bytes 38537416 | solution.py:167
  1314.3 13.9 fusion.59
  1330.7 5.8 collective-permute-done.10
  1336.5 21.0 %conditional.26 = (bf16[32,4096]{1,0:T(8,128)(2,1)}, bf16[4,32,4096]{2,1,0:T(8,128)(2,1)}) conditional(s32[]{:T(128)} %convert_element_type.230, bf16[4,32,4096]{2,1,0:T(8,128)(2,1)} %get-tuple-element.1145, (pred[32,4096]{1,0:T(8,128)(4,1)S(1)}, bf16[32,4096]{1,0:T(8,128)(2,1)S(1)}, bf16[32,4096]{1,0:T(8,128)(2,1)S(1)}, s32[]{:T(128)}, ...), branch_computations={%region_69.71_spmd, %region_70.75_spmd} | conditional | flops 1077411840 | bytes 38537416 | solution.py:167
  1341.8 13.9 fusion.73
  1375.4 80.6 %while.119 = (s32[]{:T(128)}, bf16[8,8,64,2048]{3,2,1,0:T(8,128)(2,1)}, bf16[8,128,8,64]{1,3,2,0:T(8,128)(2,1)}, s32[8,8,32]{2,1,0:T(8,128)}, bf16[128,64,64]{0,2,1:T(8,128)(2,1)S(1)}, /*index=5*/s32[]{:T(128)}) while((s32[]{:T(128)}, bf16[8,8,64,2048]{3,2,1,0:T(8,128)(2,1)}, bf16[8,128,8,64]{1,3,2,0:T(8,128)(2,1)}, ...), condition=%wide.region_78.80_spmd, body=%wide.region_77.79_spmd.sunk | while | flops 272633088 | bytes 14890569 | solution.py:195
  1379.4 6.1 fusion.280
  1389.5 6.1 fusion.280
  1399.6 6.1 fusion.280
  1409.6 6.1 fusion.280
  1419.7 6.0 fusion.280
  1429.8 6.1 fusion.280
  1439.9 6.0 fusion.280
  1449.9 6.0 fusion.280
  1456.2 132.6 %reduce-scatter.2.cloned.1.call-done = bf16[2,64,2048]{2,1,0:T(8,128)(2,1)} async-done(((bf16[64,64,2048]{2,1,0:T(8,128)(2,1)}), bf16[2,64,2048]{2,1,0:T(8,128)(2,1)}) %reduce-scatter.2.cloned.1.call-update) | async-done | bytes 524304 | tf_op jit(solution)/shard_map/reduce_scatter | solution.py:194
  1593.1 63.9 %psum.14 = f32[32]{0:T(128)S(1)} all-reduce(f32[32]{0:T(128)S(1)} %select_reduce_fusion.1), channel_id=1, replica_groups=mesh['pipe'=4,'dp'=32] {'dp'}, use_global_device_ids=true, to_apply=%region_85.87 | all-reduce | flops 32 | bytes 256 | tf_op jit(solution)/shard_map/psum | solution.py:220
  1658.3 64.2 %psum.15 = f32[]{:T(128)} all-reduce(f32[]{:T(128)} %multiply_reduce_fusion), channel_id=1, replica_groups=mesh['pipe'=4,'dp'=32] {'dp'}, use_global_device_ids=true, to_apply=%region_88.90 | all-reduce | flops 1 | bytes 8 | tf_op jit(solution)/shard_map/psum | solution.py:223
  (563 shorter events, 543.2 us)
Async XLA Ops:
  14.0 211.6 %copy-start.4 = (s32[1,64,32]{1,2,0:T(8,128)S(1)}, s32[1,64,32]{1,2,0:T(8,128)}, u32[]{:S(2)}) copy-start(s32[1,64,32]{1,2,0:T(8,128)} %param.113) | copy-start | bytes 24580
  14.0 211.6 %all-to-all-start = ((bf16[32,2,64,2048]{3,2,1,0:T(8,128)(2,1)}), bf16[32,2,64,2048]{3,2,1,0:T(8,128)(2,1)}, u32[]{:S(2)}, u32[]{:S(2)}) async-start(bf16[32,2,64,2048]{3,2,1,0:T(8,128)(2,1)} %stack.3), calls=%async_computation | async-start | bytes 33554432 | tf_op jit(solution)/shard_map/all_to_all | solution.py:13
  23.6 1565.2 %reduce-scatter.2.cloned.1.call-start = ((), (), s32[]{:S(2)}) async-start(), calls=%async_computation.2 | async-start | bytes 17301504 | tf_op jit(solution)/shard_map/reduce_scatter | solution.py:194
  225.6 0.7 copy-start.1
  307.1 2.8 copy-start
  311.0 0.7 copy-start.6
  311.7 4.9 collective-permute-start
  400.1 7.3 collective-permute-start.1
  490.5 7.3 collective-permute-start.2
  581.3 7.3 collective-permute-start.3
  589.5 89.5 %collective-permute-start.4 = (bf16[32,4096]{1,0:T(8,128)(2,1)}, bf16[32,4096]{1,0:T(8,128)(2,1)S(1)}, u32[]{:S(2)}, u32[]{:S(2)}) collective-permute-start(bf16[32,4096]{1,0:T(8,128)(2,1)} %get-tuple-element.1129), channel_id=1, source_target_pairs={{0,32},{32,64},{64,96},{1,33},{33,65},{65,97},{2,34},{34,66},{66,9... | collective-permute-start | bytes 786440 | tf_op jit(solution)/shard_map/ppermute | solution.py:19
  680.2 365.0 %collective-permute-start.5 = (bf16[32,4096]{1,0:T(8,128)(2,1)}, bf16[32,4096]{1,0:T(8,128)(2,1)S(1)}, u32[]{:S(2)}, u32[]{:S(2)}) collective-permute-start(bf16[32,4096]{1,0:T(8,128)(2,1)} %get-tuple-element.1133), channel_id=1, source_target_pairs={{0,32},{32,64},{64,96},{1,33},{33,65},{65,97},{2,34},{34,66},{66,9... | collective-permute-start | bytes 786440 | tf_op jit(solution)/shard_map/ppermute | solution.py:19
  1045.2 1.0 copy-start.2
  1047.5 83.7 %collective-permute-start.6 = (bf16[32,4096]{1,0:T(8,128)(2,1)S(1)}, bf16[32,4096]{1,0:T(8,128)(2,1)S(1)}, u32[]{:S(2)}, u32[]{:S(2)}) collective-permute-start(bf16[32,4096]{1,0:T(8,128)(2,1)S(1)} %get-tuple-element.1138), channel_id=1, source_target_pairs={{32,0},{64,32},{96,64},{33,1},{65,33},{97,65},{34,2},{66,34},{98,6... | collective-permute-start | bytes 786440 | tf_op jit(solution)/shard_map/ppermute | solution.py:19
  1131.2 7.1 collective-permute-start.7
  1138.3 143.4 %collective-permute-start.8 = (bf16[32,4096]{1,0:T(8,128)(2,1)S(1)}, bf16[32,4096]{1,0:T(8,128)(2,1)S(1)}, u32[]{:S(2)}, u32[]{:S(2)}) collective-permute-start(bf16[32,4096]{1,0:T(8,128)(2,1)S(1)} %get-tuple-element.1142), channel_id=1, source_target_pairs={{32,0},{64,32},{96,64},{33,1},{65,33},{97,65},{34,2},{66,34},{98,6... | collective-permute-start | bytes 786440 | tf_op jit(solution)/shard_map/ppermute | solution.py:19
  1302.0 7.1 collective-permute-start.9
  1329.4 7.1 collective-permute-start.10
  1357.5 7.4 collective-permute-start.11
  1456.0 132.8 %copy-start.3 = (bf16[1,2,64,2048]{3,2,1,0:T(8,128)(2,1)S(1)}, bf16[1,2,64,2048]{3,2,1,0:T(8,128)(2,1)}, u32[]{:S(2)}) copy-start(bf16[1,2,64,2048]{3,2,1,0:T(8,128)(2,1)} %param.112) | copy-start | bytes 1572868
  1456.0 132.8 %copy-start.5 = (f32[1,2,64,2048]{3,2,1,0:T(8,128)S(1)}, f32[1,2,64,2048]{3,2,1,0:T(8,128)}, u32[]{:S(2)}) copy-start(f32[1,2,64,2048]{3,2,1,0:T(8,128)} %param.115) | copy-start | bytes 3145732
Sparse Core Ops, SparseCore 0:
  1456.1 132.6 reduce-scatter.1
